TPU v7x, 32 devices: a whole 2x2x4 slice. The times are simulated.
32 devices in a mesh: ctx: 8 (over y, x, core), ch: 4 (over z).
Axes of the slice: x: 2, y: 2, z: 4, core: 2. Of those that a mesh axis runs over, the one named last changes fastest.
Arguments:
- query_act: bfloat16 [2048, 8192], P('ctx', 'ch'), may hold values from -6 to 6
- key_act: bfloat16 [2048, 8192], P('ctx', 'ch'), may hold values from -6 to 6
- value_act: bfloat16 [2048, 8192], P('ctx', 'ch'), may hold values from -6 to 6
- out_grad: bfloat16 [2048, 8192], P('ctx', 'ch'), may hold values from -6 to 6
- out_weight: bfloat16 [8192, 8192], P('ctx', 'ch'), may hold values from -0.0625 to 0.0625
- token_mask: int32 [2048], P('ctx'), may hold values from 0 to 1, as said below
- decay_rate: float32 [16, 8192], P(None, 'ch'), may hold values from 4.8828125e-05 to 0.033
- residue: float32 [16, 8192], P(None, 'ch'), may hold values from -75 to 75
Outputs:
- query_grad: bfloat16 [2048, 8192], P('ctx', 'ch')
- key_grad: bfloat16 [2048, 8192], P('ctx', 'ch')
- value_grad: bfloat16 [2048, 8192], P('ctx', 'ch')
- filter_grad: float32 [16, 8192], P(None, 'ch')
Inputs may be any that keep to these rules, and one draw needn't show every extreme that they name: `token_mask`: 1 marks a valid token; within each aligned run of 64 positions the valid tokens come first.
All inputs are finite; a program needn't handle non-finite values.
Results may differ from a plain program's by a relative error of at most 0.0015.
Values may be sent and summed in bfloat16 or wider, within the bound.
A program may use at most 192 MiB of HBM per device.

v0:
```python
import jax
import jax.numpy as jnp
from jax import lax
from jax.sharding import PartitionSpec as P


def carried_in(shard, axis, combine, identity, reverse):
    devices, here = (lax.axis_size(axis), lax.axis_index(axis))
    everything = jax.tree.map(lambda part: lax.all_gather(part, axis), shard)
    start = jax.tree.map(
        lambda part, zero: jnp.broadcast_to(jnp.asarray(zero, part.dtype), part.shape),
        shard,
        identity,
    )

    def turn(k, before):
        at = devices - 1 - k if reverse else k
        reached = at > here if reverse else at < here
        new = combine(before, jax.tree.map(lambda part: part[at], everything))
        return jax.tree.map(lambda a, b: jnp.where(reached, a, b), new, before)

    return lax.fori_loop(0, devices, turn, start)


def chain_join(earlier, later):
    return (earlier[0] * later[0], later[0] * earlier[1] + later[1])


def body(query_act, key_act, value_act, out_grad, out_weight, token_mask, decay_rate, residue):
    rows_block = 64
    tokens_here = query_act.shape[0]
    chans = query_act.shape[1]
    modes = decay_rate.shape[0]
    blocks = tokens_here // rows_block
    live = token_mask.astype(jnp.float32)[:, None]
    inputs = live * key_act.astype(jnp.float32) * value_act.astype(jnp.float32)
    root_gain = jnp.sqrt(-jnp.expm1(-2.0 * decay_rate))
    filter_gain = residue * root_gain
    places = jnp.arange(rows_block).astype(jnp.float32)[:, None, None]
    rising = jnp.exp(decay_rate[None] * places)
    falling = jnp.exp(-decay_rate[None] * places)
    step_decay = jnp.exp(-decay_rate)
    trailing = jnp.exp(-decay_rate[None] * (rows_block - places))
    row_ids = lax.broadcasted_iota(jnp.int32, (rows_block, rows_block), 0)
    col_ids = lax.broadcasted_iota(jnp.int32, (rows_block, rows_block), 1)
    lower_ones = (row_ids >= col_ids).astype(jnp.float32)
    upper_ones = (row_ids <= col_ids).astype(jnp.float32)
    zeros = jnp.zeros((modes, chans), jnp.float32)

    def forward_block(carried, block_in):
        scaled = (rising * block_in[:, None, :]).reshape(rows_block, modes * chans)
        summed = jnp.dot(lower_ones, scaled, precision=lax.Precision.HIGHEST).reshape(
            rows_block, modes, chans
        )
        states = falling * summed + falling * step_decay[None] * carried[None]
        return (states[-1], jnp.sum(filter_gain[None] * states, axis=1))

    end_state, conv_local = lax.scan(
        forward_block, zeros, inputs.reshape(blocks, rows_block, chans)
    )
    conv_local = conv_local.reshape(tokens_here, chans)
    full_grad = lax.all_gather(out_grad, "ch", axis=1, tiled=True)
    gate_grad = jnp.dot(
        full_grad,
        lax.all_gather(out_weight, "ctx", axis=0, tiled=True),
        preferred_element_type=jnp.float32,
    )
    conv_grad = gate_grad * query_act.astype(jnp.float32)

    def backward_block(carry, block_in):
        carried, running = carry
        grad_blk, input_blk = block_in
        scaled = (falling * grad_blk[:, None, :]).reshape(rows_block, modes * chans)
        summed = jnp.dot(upper_ones, scaled, precision=lax.Precision.HIGHEST).reshape(
            rows_block, modes, chans
        )
        states = rising * summed + trailing * carried[None]
        running = running + jnp.sum(input_blk[:, None, :] * states, axis=0)
        return ((states[0], running), jnp.sum(filter_gain[None] * states, axis=1))

    (start_state, filter_local), grad_local = lax.scan(
        backward_block,
        (zeros, zeros),
        (conv_grad.reshape(blocks, rows_block, chans), inputs.reshape(blocks, rows_block, chans)),
        reverse=True,
    )
    grad_local = grad_local.reshape(tokens_here, chans)
    span_decay = jnp.exp(-decay_rate * tokens_here)
    forward_in = carried_in(
        (span_decay, end_state), "ctx", chain_join, (jnp.ones_like(span_decay), zeros), False
    )[1]
    backward_in = carried_in(
        (span_decay, start_state), "ctx", chain_join, (jnp.ones_like(span_decay), zeros), True
    )[1]
    token_places = jnp.arange(tokens_here).astype(jnp.float32)[:, None, None]
    conv = conv_local + jnp.sum(
        jnp.exp(-decay_rate[None] * (token_places + 1.0)) * (filter_gain * forward_in)[None], axis=1
    )
    input_grad = grad_local + jnp.sum(
        jnp.exp(-decay_rate[None] * (tokens_here - token_places))
        * (filter_gain * backward_in)[None],
        axis=1,
    )
    query_grad = (gate_grad * conv).astype(jnp.bfloat16)
    key_grad = (live * input_grad * value_act.astype(jnp.float32)).astype(jnp.bfloat16)
    value_grad = (live * input_grad * key_act.astype(jnp.float32)).astype(jnp.bfloat16)
    filter_terms = root_gain * (filter_local + backward_in * step_decay * end_state)
    filter_grad = lax.psum(filter_terms, "ctx")
    return (query_grad, key_grad, value_grad, filter_grad)


def solution(mesh):
    placed = (
        P("ctx", "ch"),
        P("ctx", "ch"),
        P("ctx", "ch"),
        P("ctx", "ch"),
        P("ctx", "ch"),
        P("ctx"),
        P(None, "ch"),
        P(None, "ch"),
    )
    return jax.shard_map(
        body,
        mesh=mesh,
        in_specs=placed,
        out_specs=(P("ctx", "ch"), P("ctx", "ch"), P("ctx", "ch"), P(None, "ch")),
        check_vma=False,
    )
```

profile of v0, /device:TPU:0, one launch (start us, length us, event | category | flops | bytes accessed | tf_op | source)
XLA Modules:
  0.0 719.4 jit_solution(11028100770254350850)
XLA Ops:
  14.7 100.9 %while.67 = (s32[]{:T(128)}, f32[16,2048]{1,0:T(8,128)S(1)}, f32[4,64,2048]{2,1,0:T(8,128)}, f32[4,64,2048]{2,1,0:T(8,128)S(1)}, f32[16,2048]{1,0:T(8,128)S(1)},...) while((s32[]{:T(128)}, f32[16,2048]{1,0:T(8,128)S(1)}, ...), condition=%wide.region_2.3_spmd.clone.clone, body=%wide.region_0.2_spmd.clone.clone.sunk | while | flops 1629364224 | bytes 79561336 | solution.py:58
  21.2 8.5 %fusion.52 = f32[32768,64]{0,1:T(8,128)S(1)} fusion(f32[64,32768]{1,0:T(8,128)S(1)} %bitcast.141), kind=kOutput, calls=%fused_computation.23.clone.1 | convolution fusion | flops 1610620928 | bytes 16777216 | tf_op jit(solution)/shard_map/while/body/eval_jaxpr/dot_general | solution.py:52
  71.5 8.5 %fusion.52 = f32[32768,64]{0,1:T(8,128)S(1)} fusion(f32[64,32768]{1,0:T(8,128)S(1)} %bitcast.141), kind=kOutput, calls=%fused_computation.23.clone.1 | convolution fusion | flops 1610620928 | bytes 16777216 | tf_op jit(solution)/shard_map/while/body/eval_jaxpr/dot_general | solution.py:52
  96.6 8.5 %fusion.52 = f32[32768,64]{0,1:T(8,128)S(1)} fusion(f32[64,32768]{1,0:T(8,128)S(1)} %bitcast.141), kind=kOutput, calls=%fused_computation.23.clone.1 | convolution fusion | flops 1610620928 | bytes 16777216 | tf_op jit(solution)/shard_map/while/body/eval_jaxpr/dot_general | solution.py:52
  117.6 136.5 %all-gather.11.cloned.1.call-done = bf16[8192,2048]{1,0:T(8,128)(2,1)} async-done(((bf16[1024,2048]{1,0:T(8,128)(2,1)}), bf16[8192,2048]{1,0:T(8,128)(2,1)}) %all-gather.11.cloned.1.call-update) | async-done | bytes 33554448 | tf_op jit(solution)/shard_map/all_gather | solution.py:65
  254.1 17.9 %convert_multiply_fusion.4 = (f32[256,2048]{1,0:T(8,128)}, f32[256,2048]{1,0:T(8,128)}) fusion(bf16[256,2048]{1,0:T(8,128)(2,1)} %param.16, bf16[256,8192]{1,0:T(8,128)(2,1)} %all-gather.9.cloned.1.call-done, bf16[8192,2048]{1,0:T(8,128)(2,1)} %all-gather.11.cloned.1.call-done), kind=kOutput, calls=%fused_computation.57 | convolution fusion | flops 8590983168 | bytes 42991616 | tf_op jit(solution)/shard_map/dot_general | solution.py:63
  274.3 343.8 %while.68 = (s32[]{:T(128)}, f32[16,2048]{1,0:T(8,128)}, f32[16,2048]{1,0:T(8,128)}, f32[4,64,2048]{2,1,0:T(8,128)}, f32[4,64,2048]{2,1,0:T(8,128)}, /*index=5*/...) while((s32[]{:T(128)}, f32[16,2048]{1,0:T(8,128)}, ...), condition=%wide.region_9.10_spmd.clone.clone.clone, body=%wide.region_6.0_spmd.clone.clone.clone.sunk | while | flops 1639882752 | bytes 212862208 | solution.py:81
  283.5 8.8 %fusion.55 = f32[32768,64]{0,1:T(8,128)S(1)} fusion(f32[64,32768]{1,0:T(8,128)S(1)} %bitcast.143), kind=kOutput, calls=%fused_computation.41.clone.1 | convolution fusion | flops 1610620928 | bytes 16777216 | tf_op jit(solution)/shard_map/while/body/eval_jaxpr/dot_general | solution.py:74
  300.3 10.9 %multiply_reduce_fusion.7 = (f32[64,2048]{1,0:T(8,128)S(1)}, f32[64,16,2048]{2,1,0:T(8,128)}, f32[64,16,2048]{2,1,0:T(8,128)S(1)}, f32[64,16,2048]{2,1,0:T(8,128)}) fusion(f32[16,2048]{1,0:T(8,128)} %copy-done.7, f32[16,2048]{1,0:T(8,128)} %get-tuple-element.1005, f32[64]{0:T(128)S(1)} %get-tuple-element.1028, f32[16,2048]{1,0:T(8,128)} %copy-done, ...), kind=kLoop, calls=%fused_computation.35.clone.1 | loop fusion | flops 14548992 | bytes 34603520 | tf_op jit(solution)/shard_map/while/body/eval_jaxpr/reduce_sum | solution.py:79
  317.1 11.7 %copy.32 = f32[8,8,16,2048]{3,1,2,0:T(8,128)} copy(f32[8,8,16,2048]{3,2,1,0:T(8,128)} %bitcast.148) | data formatting | bytes 16777216 | tf_op jit(solution)/shard_map/while
  328.7 11.7 %copy.33 = f32[8,8,16,2048]{3,1,2,0:T(8,128)} copy(f32[8,8,16,2048]{3,2,1,0:T(8,128)} %bitcast.145) | data formatting | bytes 16777216 | tf_op jit(solution)/shard_map/while
  348.6 9.5 %fusion.56 = f32[32768]{0:T(1024)S(1)} fusion(f32[64,32768]{1,0:T(8,128)} %bitcast.149, f32[64,32768]{1,0:T(8,128)} %bitcast.150, f32[32768,64]{0,1:T(8,128)S(1)} %fusion.55, f32[64,32768]{1,0:T(8,128)} %bitcast.151, f32[32768]{0:T(1024)S(1)} %bitcast.153), kind=kLoop, calls=%fused_computation.31.clone.1 | loop fusion | flops 10452992 | bytes 33816576 | tf_op jit(solution)/shard_map/while/body/eval_jaxpr/reduce_sum | solution.py:78
  368.4 9.0 %fusion.55 = f32[32768,64]{0,1:T(8,128)S(1)} fusion(f32[64,32768]{1,0:T(8,128)S(1)} %bitcast.143), kind=kOutput, calls=%fused_computation.41.clone.1 | convolution fusion | flops 1610620928 | bytes 16777216 | tf_op jit(solution)/shard_map/while/body/eval_jaxpr/dot_general | solution.py:74
  385.4 10.7 %multiply_reduce_fusion.7 = (f32[64,2048]{1,0:T(8,128)S(1)}, f32[64,16,2048]{2,1,0:T(8,128)}, f32[64,16,2048]{2,1,0:T(8,128)S(1)}, f32[64,16,2048]{2,1,0:T(8,128)}) fusion(f32[16,2048]{1,0:T(8,128)} %copy-done.7, f32[16,2048]{1,0:T(8,128)} %get-tuple-element.1005, f32[64]{0:T(128)S(1)} %get-tuple-element.1028, f32[16,2048]{1,0:T(8,128)} %copy-done, ...), kind=kLoop, calls=%fused_computation.35.clone.1 | loop fusion | flops 14548992 | bytes 34603520 | tf_op jit(solution)/shard_map/while/body/eval_jaxpr/reduce_sum | solution.py:79
  402.0 11.7 %copy.32 = f32[8,8,16,2048]{3,1,2,0:T(8,128)} copy(f32[8,8,16,2048]{3,2,1,0:T(8,128)} %bitcast.148) | data formatting | bytes 16777216 | tf_op jit(solution)/shard_map/while
  413.6 11.7 %copy.33 = f32[8,8,16,2048]{3,1,2,0:T(8,128)} copy(f32[8,8,16,2048]{3,2,1,0:T(8,128)} %bitcast.145) | data formatting | bytes 16777216 | tf_op jit(solution)/shard_map/while
  433.6 9.5 %fusion.56 = f32[32768]{0:T(1024)S(1)} fusion(f32[64,32768]{1,0:T(8,128)} %bitcast.149, f32[64,32768]{1,0:T(8,128)} %bitcast.150, f32[32768,64]{0,1:T(8,128)S(1)} %fusion.55, f32[64,32768]{1,0:T(8,128)} %bitcast.151, f32[32768]{0:T(1024)S(1)} %bitcast.153), kind=kLoop, calls=%fused_computation.31.clone.1 | loop fusion | flops 10452992 | bytes 33816576 | tf_op jit(solution)/shard_map/while/body/eval_jaxpr/reduce_sum | solution.py:78
  453.5 8.8 %fusion.55 = f32[32768,64]{0,1:T(8,128)S(1)} fusion(f32[64,32768]{1,0:T(8,128)S(1)} %bitcast.143), kind=kOutput, calls=%fused_computation.41.clone.1 | convolution fusion | flops 1610620928 | bytes 16777216 | tf_op jit(solution)/shard_map/while/body/eval_jaxpr/dot_general | solution.py:74
  470.2 10.7 %multiply_reduce_fusion.7 = (f32[64,2048]{1,0:T(8,128)S(1)}, f32[64,16,2048]{2,1,0:T(8,128)}, f32[64,16,2048]{2,1,0:T(8,128)S(1)}, f32[64,16,2048]{2,1,0:T(8,128)}) fusion(f32[16,2048]{1,0:T(8,128)} %copy-done.7, f32[16,2048]{1,0:T(8,128)} %get-tuple-element.1005, f32[64]{0:T(128)S(1)} %get-tuple-element.1028, f32[16,2048]{1,0:T(8,128)} %copy-done, ...), kind=kLoop, calls=%fused_computation.35.clone.1 | loop fusion | flops 14548992 | bytes 34603520 | tf_op jit(solution)/shard_map/while/body/eval_jaxpr/reduce_sum | solution.py:79
  486.8 11.7 %copy.32 = f32[8,8,16,2048]{3,1,2,0:T(8,128)} copy(f32[8,8,16,2048]{3,2,1,0:T(8,128)} %bitcast.148) | data formatting | bytes 16777216 | tf_op jit(solution)/shard_map/while
  498.5 11.7 %copy.33 = f32[8,8,16,2048]{3,1,2,0:T(8,128)} copy(f32[8,8,16,2048]{3,2,1,0:T(8,128)} %bitcast.145) | data formatting | bytes 16777216 | tf_op jit(solution)/shard_map/while
  518.6 9.5 %fusion.56 = f32[32768]{0:T(1024)S(1)} fusion(f32[64,32768]{1,0:T(8,128)} %bitcast.149, f32[64,32768]{1,0:T(8,128)} %bitcast.150, f32[32768,64]{0,1:T(8,128)S(1)} %fusion.55, f32[64,32768]{1,0:T(8,128)} %bitcast.151, f32[32768]{0:T(1024)S(1)} %bitcast.153), kind=kLoop, calls=%fused_computation.31.clone.1 | loop fusion | flops 10452992 | bytes 33816576 | tf_op jit(solution)/shard_map/while/body/eval_jaxpr/reduce_sum | solution.py:78
  538.3 8.8 %fusion.55 = f32[32768,64]{0,1:T(8,128)S(1)} fusion(f32[64,32768]{1,0:T(8,128)S(1)} %bitcast.143), kind=kOutput, calls=%fused_computation.41.clone.1 | convolution fusion | flops 1610620928 | bytes 16777216 | tf_op jit(solution)/shard_map/while/body/eval_jaxpr/dot_general | solution.py:74
  555.1 10.9 %multiply_reduce_fusion.7 = (f32[64,2048]{1,0:T(8,128)S(1)}, f32[64,16,2048]{2,1,0:T(8,128)}, f32[64,16,2048]{2,1,0:T(8,128)S(1)}, f32[64,16,2048]{2,1,0:T(8,128)}) fusion(f32[16,2048]{1,0:T(8,128)} %copy-done.7, f32[16,2048]{1,0:T(8,128)} %get-tuple-element.1005, f32[64]{0:T(128)S(1)} %get-tuple-element.1028, f32[16,2048]{1,0:T(8,128)} %copy-done, ...), kind=kLoop, calls=%fused_computation.35.clone.1 | loop fusion | flops 14548992 | bytes 34603520 | tf_op jit(solution)/shard_map/while/body/eval_jaxpr/reduce_sum | solution.py:79
  571.9 11.7 %copy.32 = f32[8,8,16,2048]{3,1,2,0:T(8,128)} copy(f32[8,8,16,2048]{3,2,1,0:T(8,128)} %bitcast.148) | data formatting | bytes 16777216 | tf_op jit(solution)/shard_map/while
  583.5 11.7 %copy.33 = f32[8,8,16,2048]{3,1,2,0:T(8,128)} copy(f32[8,8,16,2048]{3,2,1,0:T(8,128)} %bitcast.145) | data formatting | bytes 16777216 | tf_op jit(solution)/shard_map/while
  603.4 9.5 %fusion.56 = f32[32768]{0:T(1024)S(1)} fusion(f32[64,32768]{1,0:T(8,128)} %bitcast.149, f32[64,32768]{1,0:T(8,128)} %bitcast.150, f32[32768,64]{0,1:T(8,128)S(1)} %fusion.55, f32[64,32768]{1,0:T(8,128)} %bitcast.151, f32[32768]{0:T(1024)S(1)} %bitcast.153), kind=kLoop, calls=%fused_computation.31.clone.1 | loop fusion | flops 10452992 | bytes 33816576 | tf_op jit(solution)/shard_map/while/body/eval_jaxpr/reduce_sum | solution.py:78
  618.2 13.6 %while.65 = (s32[]{:T(128)}, f32[16,2048]{1,0:T(8,128)}, s32[]{:T(128)}, f32[8,16,2048]{2,1,0:T(8,128)}, f32[8,16,2048]{2,1,0:T(8,128)}, /*index=5*/s32[]{:T(128)}, s32[]{:T(128)}) while((s32[]{:T(128)}, f32[16,2048]{1,0:T(8,128)}, s32[]{:T(128)}, f32[8,16,2048]{2,1,0:T(8,128)}, f32[8,16,2048]{2,1,0:T(8,128)}, ...), condition=%wide.region_4.5_spmd.clone, body=%wide.region_3.4_spmd.clone.sunk | while | flops 131076 | bytes 524397 | solution.py:22
  631.8 9.8 %all-gather.17.cloned.1.call-done = f32[128,2048]{1,0:T(8,128)} async-done(((f32[16,2048]{1,0:T(8,128)}), f32[128,2048]{1,0:T(8,128)}) %all-gather.17.cloned.1.call-update) | async-done | bytes 1048592 | tf_op jit(solution)/shard_map/all_gather | solution.py:9
  641.6 13.5 %while.66 = (s32[]{:T(128)}, f32[16,2048]{1,0:T(8,128)}, s32[]{:T(128)}, f32[8,16,2048]{2,1,0:T(8,128)}, f32[8,16,2048]{2,1,0:T(8,128)}, /*index=5*/s32[]{:T(128)}, s32[]{:T(128)}, s32[]{:T(128)}, s32[]{:T(128)}) while((s32[]{:T(128)}, f32[16,2048]{1,0:T(8,128)}, s32[]{:T(128)}, f32[8,16,2048]{2,1,0:T(8,128)}, ...), condition=%wide.region_11.12_spmd.clone, body=%wide.region_10.11_spmd.clone.sunk | while | flops 131080 | bytes 524459 | solution.py:22
  657.1 21.9 %multiply_reduce_fusion.2 = (f32[256,2048]{1,0:T(8,128)S(1)}, f32[256,2048]{1,0:T(8,128)S(1)}) fusion(f32[16,2048]{1,0:T(8,128)S(1)} %get-tuple-element.781, f32[256]{0:T(256)S(1)} %copy-done.20, f32[16,2048]{1,0:T(8,128)S(1)} %get-tuple-element.1121, f32[16,2048]{1,0:T(8,128)S(1)} %get-tuple-element.782, f32[256]{0:T(256)} %convert_add_fusion), kind=kLoop, calls=%fused_computation.44 | loop fusion | flops 49283072 | bytes 4589568 | tf_op jit(solution)/shard_map/reduce_sum | solution.py:99
  682.1 28.6 %all-reduce.2.cloned.1.call-done = f32[16,2048]{1,0:T(8,128)} async-done(((f32[16,2048]{1,0:T(8,128)}), f32[16,2048]{1,0:T(8,128)}) %all-reduce.2.cloned.1.call-update) | async-done | bytes 131088 | tf_op jit(solution)/shard_map/psum | solution.py:108
  (229 shorter events, 248.1 us)
Async XLA Ops:
  7.2 110.4 %all-gather.9.cloned.1.call-start = ((), (), s32[]{:S(2)}) async-start(), calls=%async_computation | async-start | bytes 5242880 | tf_op jit(solution)/shard_map/all_gather | solution.py:62
  7.9 246.2 %all-gather.11.cloned.1.call-start = ((), (), s32[]{:S(2)}) async-start(), calls=%async_computation.1 | async-start | bytes 37748736 | tf_op jit(solution)/shard_map/all_gather | solution.py:65
  8.7 609.5 %all-gather.13.cloned.1.call-start = ((), (), s32[]{:S(2)}) async-start(), calls=%async_computation.3 | async-start | bytes 1179648 | tf_op jit(solution)/shard_map/all_gather | solution.py:9
  10.5 607.8 %all-gather.15.cloned.1.call-start = ((), (), s32[]{:S(2)}) async-start(), calls=%async_computation.4 | async-start | bytes 1179648 | tf_op jit(solution)/shard_map/all_gather | solution.py:9
  116.3 525.3 %all-gather.17.cloned.1.call-start = ((), (), s32[]{:S(2)}) async-start(), calls=%async_computation.5 | async-start | bytes 1179648 | tf_op jit(solution)/shard_map/all_gather | solution.py:9
  274.3 382.7 %copy-start.20 = (f32[256]{0:T(256)S(1)}, f32[256]{0:T(256)}, u32[]{:S(2)}) copy-start(f32[256]{0:T(256)} %convert_subtract_fusion) | copy-start | bytes 3076
  348.6 9.5 %copy-start.13 = (f32[16,2048]{1,0:T(8,128)S(1)}, f32[16,2048]{1,0:T(8,128)}, u32[]{:S(2)}) copy-start(f32[16,2048]{1,0:T(8,128)} %get-tuple-element.1006) | copy-start | bytes 393220 | tf_op jit(solution)/shard_map/while
  348.6 10.5 %copy-start.1 = (f32[16,2048]{1,0:T(8,128)S(1)}, f32[16,2048]{1,0:T(8,128)}, u32[]{:S(2)}) copy-start(f32[16,2048]{1,0:T(8,128)} %copy-done) | copy-start | bytes 393220 | tf_op jit(solution)/shard_map/while
  348.6 10.5 %copy-start.3 = (f32[4,64,2048]{2,1,0:T(8,128)S(1)}, f32[4,64,2048]{2,1,0:T(8,128)}, u32[]{:S(2)}) copy-start(f32[4,64,2048]{2,1,0:T(8,128)} %copy-done.2) | copy-start | bytes 6291460 | tf_op jit(solution)/shard_map/while
  348.6 10.5 %copy-start.6 = (f32[16,2048]{1,0:T(8,128)S(1)}, f32[16,2048]{1,0:T(8,128)}, u32[]{:S(2)}) copy-start(f32[16,2048]{1,0:T(8,128)} %copy-done.5) | copy-start | bytes 393220 | tf_op jit(solution)/shard_map/while
  348.6 10.5 %copy-start.8 = (f32[16,2048]{1,0:T(8,128)S(1)}, f32[16,2048]{1,0:T(8,128)}, u32[]{:S(2)}) copy-start(f32[16,2048]{1,0:T(8,128)} %copy-done.7) | copy-start | bytes 393220 | tf_op jit(solution)/shard_map/while
  433.5 9.5 %copy-start.13 = (f32[16,2048]{1,0:T(8,128)S(1)}, f32[16,2048]{1,0:T(8,128)}, u32[]{:S(2)}) copy-start(f32[16,2048]{1,0:T(8,128)} %get-tuple-element.1006) | copy-start | bytes 393220 | tf_op jit(solution)/shard_map/while
  433.5 10.5 %copy-start.1 = (f32[16,2048]{1,0:T(8,128)S(1)}, f32[16,2048]{1,0:T(8,128)}, u32[]{:S(2)}) copy-start(f32[16,2048]{1,0:T(8,128)} %copy-done) | copy-start | bytes 393220 | tf_op jit(solution)/shard_map/while
  433.5 10.5 %copy-start.3 = (f32[4,64,2048]{2,1,0:T(8,128)S(1)}, f32[4,64,2048]{2,1,0:T(8,128)}, u32[]{:S(2)}) copy-start(f32[4,64,2048]{2,1,0:T(8,128)} %copy-done.2) | copy-start | bytes 6291460 | tf_op jit(solution)/shard_map/while
  433.5 10.5 %copy-start.6 = (f32[16,2048]{1,0:T(8,128)S(1)}, f32[16,2048]{1,0:T(8,128)}, u32[]{:S(2)}) copy-start(f32[16,2048]{1,0:T(8,128)} %copy-done.5) | copy-start | bytes 393220 | tf_op jit(solution)/shard_map/while
  433.5 10.5 %copy-start.8 = (f32[16,2048]{1,0:T(8,128)S(1)}, f32[16,2048]{1,0:T(8,128)}, u32[]{:S(2)}) copy-start(f32[16,2048]{1,0:T(8,128)} %copy-done.7) | copy-start | bytes 393220 | tf_op jit(solution)/shard_map/while
  518.6 9.5 %copy-start.13 = (f32[16,2048]{1,0:T(8,128)S(1)}, f32[16,2048]{1,0:T(8,128)}, u32[]{:S(2)}) copy-start(f32[16,2048]{1,0:T(8,128)} %get-tuple-element.1006) | copy-start | bytes 393220 | tf_op jit(solution)/shard_map/while
  518.6 10.4 %copy-start.1 = (f32[16,2048]{1,0:T(8,128)S(1)}, f32[16,2048]{1,0:T(8,128)}, u32[]{:S(2)}) copy-start(f32[16,2048]{1,0:T(8,128)} %copy-done) | copy-start | bytes 393220 | tf_op jit(solution)/shard_map/while
  518.6 10.4 %copy-start.3 = (f32[4,64,2048]{2,1,0:T(8,128)S(1)}, f32[4,64,2048]{2,1,0:T(8,128)}, u32[]{:S(2)}) copy-start(f32[4,64,2048]{2,1,0:T(8,128)} %copy-done.2) | copy-start | bytes 6291460 | tf_op jit(solution)/shard_map/while
  518.6 10.4 %copy-start.6 = (f32[16,2048]{1,0:T(8,128)S(1)}, f32[16,2048]{1,0:T(8,128)}, u32[]{:S(2)}) copy-start(f32[16,2048]{1,0:T(8,128)} %copy-done.5) | copy-start | bytes 393220 | tf_op jit(solution)/shard_map/while
  518.6 10.4 %copy-start.8 = (f32[16,2048]{1,0:T(8,128)S(1)}, f32[16,2048]{1,0:T(8,128)}, u32[]{:S(2)}) copy-start(f32[16,2048]{1,0:T(8,128)} %copy-done.7) | copy-start | bytes 393220 | tf_op jit(solution)/shard_map/while
  603.4 10.5 %copy-start.1 = (f32[16,2048]{1,0:T(8,128)S(1)}, f32[16,2048]{1,0:T(8,128)}, u32[]{:S(2)}) copy-start(f32[16,2048]{1,0:T(8,128)} %copy-done) | copy-start | bytes 393220 | tf_op jit(solution)/shard_map/while
  603.4 10.5 %copy-start.3 = (f32[4,64,2048]{2,1,0:T(8,128)S(1)}, f32[4,64,2048]{2,1,0:T(8,128)}, u32[]{:S(2)}) copy-start(f32[4,64,2048]{2,1,0:T(8,128)} %copy-done.2) | copy-start | bytes 6291460 | tf_op jit(solution)/shard_map/while
  603.4 10.5 %copy-start.6 = (f32[16,2048]{1,0:T(8,128)S(1)}, f32[16,2048]{1,0:T(8,128)}, u32[]{:S(2)}) copy-start(f32[16,2048]{1,0:T(8,128)} %copy-done.5) | copy-start | bytes 393220 | tf_op jit(solution)/shard_map/while
  603.4 10.5 %copy-start.8 = (f32[16,2048]{1,0:T(8,128)S(1)}, f32[16,2048]{1,0:T(8,128)}, u32[]{:S(2)}) copy-start(f32[16,2048]{1,0:T(8,128)} %copy-done.7) | copy-start | bytes 393220 | tf_op jit(solution)/shard_map/while
  618.1 92.5 %all-reduce.2.cloned.1.call-start = ((), (), s32[]{:S(2)}) async-start(), calls=%async_computation.2 | async-start | bytes 262144 | tf_op jit(solution)/shard_map/psum | solution.py:108
  657.0 22.0 %copy-start.11 = (f32[4,64,2048]{2,1,0:T(8,128)S(1)}, f32[4,64,2048]{2,1,0:T(8,128)}, u32[]{:S(2)}) copy-start(f32[4,64,2048]{2,1,0:T(8,128)} %get-tuple-element.500) | copy-start | bytes 6291460
  657.0 22.0 %copy-start.12 = (f32[4,64,2048]{2,1,0:T(8,128)S(1)}, f32[4,64,2048]{2,1,0:T(8,128)}, u32[]{:S(2)}) copy-start(f32[4,64,2048]{2,1,0:T(8,128)} %get-tuple-element.497) | copy-start | bytes 6291460
  657.1 22.0 %copy-start.15 = (bf16[256,2048]{1,0:T(8,128)(2,1)S(1)}, bf16[256,2048]{1,0:T(8,128)(2,1)}, u32[]{:S(2)}) copy-start(bf16[256,2048]{1,0:T(8,128)(2,1)} %param.17) | copy-start | bytes 3145732
  657.1 22.0 %copy-start.16 = (bf16[256,2048]{1,0:T(8,128)(2,1)S(1)}, bf16[256,2048]{1,0:T(8,128)(2,1)}, u32[]{:S(2)}) copy-start(bf16[256,2048]{1,0:T(8,128)(2,1)} %param.18) | copy-start | bytes 3145732
  657.1 22.0 %copy-start.17 = (f32[256,2048]{1,0:T(8,128)S(1)}, f32[256,2048]{1,0:T(8,128)}, u32[]{:S(2)}) copy-start(f32[256,2048]{1,0:T(8,128)} %get-tuple-element.788) | copy-start | bytes 6291460
  657.1 22.0 %copy-start.19 = (f32[256]{0:T(256)S(1)}, f32[256]{0:T(256)}, u32[]{:S(2)}) copy-start(f32[256]{0:T(256)} %copy-done.18) | copy-start | bytes 3076
  (28 other events, 124.1 us)
Sparse Core Ops, SparseCore 0:
  9.6 83.4 all-gather.8
  94.9 159.1 all-gather.10
  256.6 23.3 all-gather.12
  282.3 23.3 all-gather.14
  618.2 23.3 all-gather.16
  657.1 53.4 all-reduce.1
where the time goes:
time: 721 us; the launch traced here: 719 us
  local copies, waits for them, and re-layouts  266 us (37%)
  waiting for transfers between devices  176 us (24%)
  other arithmetic  169 us (23%)
  matrix products  87.4 us (12%)
  between operations  14.7 us (2%)
    while x120, local copies, waits for them, and re-layouts  225 us
    all_gather x1, waiting for transfers between devices, body(): lax.all_gather(out_weight, 'ctx', axis=0, tiled=True)  137 us
    reduce_sum x4, other arithmetic, backward_block(): return ((states[0], running), jnp.sum(filter_gain[None] * states, axis=1))  43.2 us
    reduce_sum x4, other arithmetic, backward_block(): running = running + jnp.sum(input_blk[:, None, :] * states, axis=0)  37.9 us
    dot_general x4, matrix products, backward_block(): jnp.dot(upper_ones, scaled, precision=lax.Precision.HIGHEST)  35.5 us
    dot_general x4, matrix products, forward_block(): jnp.dot(lower_ones, scaled, precision=lax.Precision.HIGHEST)  34 us
    psum x1, waiting for transfers between devices, body(): filter_grad = lax.psum(filter_terms, 'ctx')  28.6 us
    select_n x16, other arithmetic, turn(): return jax.tree.map(lambda a, b: jnp.where(reached, a, b), new, before)  27.1 us
  transfers between devices with their start and end apart: 6, of which 3 were waited for; matrix products, arithmetic and copies ran while one was open for 70% of the time, Pallas kernels for 0%

commit v1 on v0

--- a/solution.py
+++ b/solution.py
@@ -2,6 +2,7 @@
 import jax.numpy as jnp
 from jax import lax
 from jax.sharding import PartitionSpec as P
+from jax.lax import all_gather
 
 
 def carried_in(shard, axis, combine, identity, reverse):
@@ -27,6 +28,10 @@
 
 
 def body(query_act, key_act, value_act, out_grad, out_weight, token_mask, decay_rate, residue):
+
+    def use_links(local_values):
+        return all_gather(local_values, "ctx").sum(axis=0)
+
     rows_block = 64
     tokens_here = query_act.shape[0]
     chans = query_act.shape[1]
@@ -105,7 +110,7 @@
     key_grad = (live * input_grad * value_act.astype(jnp.float32)).astype(jnp.bfloat16)
     value_grad = (live * input_grad * key_act.astype(jnp.float32)).astype(jnp.bfloat16)
     filter_terms = root_gain * (filter_local + backward_in * step_decay * end_state)
-    filter_grad = lax.psum(filter_terms, "ctx")
+    filter_grad = use_links(filter_terms)
     return (query_grad, key_grad, value_grad, filter_grad)
 
 

time: 721 us -> 693 us (0.961)
  waiting for transfers between devices: 176 us -> 148 us
    psum x1 -> x0, waiting for transfers between devices: 28.6 us -> none  [body(): filter_grad = lax.psum(filter_terms, 'ctx')]
  transfers between devices with their start and end apart: 6 -> 6, of which waited for: 3 -> 2; matrix products, arithmetic and copies ran while one was open for 70% -> 73% of each run, Pallas kernels for 0% -> 0%
where the time goes in v1:
time: 693 us; the launch traced here: 691 us
  local copies, waits for them, and re-layouts  264 us (38%)
  other arithmetic  170 us (25%)
  waiting for transfers between devices  148 us (21%)
  matrix products  87.4 us (13%)
  between operations  14.7 us (2%)
    while x120, local copies, waits for them, and re-layouts  225 us
    all_gather x1, waiting for transfers between devices, body(): lax.all_gather(out_weight, 'ctx', axis=0, tiled=True)  137 us
    reduce_sum x4, other arithmetic, backward_block(): return ((states[0], running), jnp.sum(filter_gain[None] * states, axis=1))  43.2 us
    reduce_sum x4, other arithmetic, backward_block(): running = running + jnp.sum(input_blk[:, None, :] * states, axis=0)  37.9 us
    dot_general x4, matrix products, backward_block(): jnp.dot(upper_ones, scaled, precision=lax.Precision.HIGHEST)  35.5 us
    dot_general x4, matrix products, forward_block(): jnp.dot(lower_ones, scaled, precision=lax.Precision.HIGHEST)  34 us
    select_n x16, other arithmetic, turn(): return jax.tree.map(lambda a, b: jnp.where(reached, a, b), new, before)  27.1 us
    reduce_sum x1, other arithmetic, body(): jnp.sum(jnp.exp(-decay_rate[None] * (tokens_here - token_places)) * (filt...  21.9 us
  transfers between devices with their start and end apart: 6, of which 2 were waited for; matrix products, arithmetic and copies ran while one was open for 73% of the time, Pallas kernels for 0%

profile of v1, /device:TPU:0, one launch (start us, length us, event | category | flops | bytes accessed | tf_op | source)
XLA Modules:
  0.0 691.3 jit_solution(15695479811932601320)
XLA Ops:
  14.7 100.9 %while.67 = (s32[]{:T(128)}, f32[16,2048]{1,0:T(8,128)S(1)}, f32[4,64,2048]{2,1,0:T(8,128)}, f32[4,64,2048]{2,1,0:T(8,128)S(1)}, f32[16,2048]{1,0:T(8,128)S(1)},...) while((s32[]{:T(128)}, f32[16,2048]{1,0:T(8,128)S(1)}, ...), condition=%wide.region_2.3_spmd.clone.clone, body=%wide.region_0.2_spmd.clone.clone.sunk | while | flops 1629364224 | bytes 79561336 | solution.py:63
  21.2 8.5 %fusion.52 = f32[32768,64]{0,1:T(8,128)S(1)} fusion(f32[64,32768]{1,0:T(8,128)S(1)} %bitcast.142), kind=kOutput, calls=%fused_computation.23.clone.1 | convolution fusion | flops 1610620928 | bytes 16777216 | tf_op jit(solution)/shard_map/while/body/eval_jaxpr/dot_general | solution.py:57
  46.3 8.5 %fusion.52 = f32[32768,64]{0,1:T(8,128)S(1)} fusion(f32[64,32768]{1,0:T(8,128)S(1)} %bitcast.142), kind=kOutput, calls=%fused_computation.23.clone.1 | convolution fusion | flops 1610620928 | bytes 16777216 | tf_op jit(solution)/shard_map/while/body/eval_jaxpr/dot_general | solution.py:57
  71.5 8.5 %fusion.52 = f32[32768,64]{0,1:T(8,128)S(1)} fusion(f32[64,32768]{1,0:T(8,128)S(1)} %bitcast.142), kind=kOutput, calls=%fused_computation.23.clone.1 | convolution fusion | flops 1610620928 | bytes 16777216 | tf_op jit(solution)/shard_map/while/body/eval_jaxpr/dot_general | solution.py:57
  96.6 8.5 %fusion.52 = f32[32768,64]{0,1:T(8,128)S(1)} fusion(f32[64,32768]{1,0:T(8,128)S(1)} %bitcast.142), kind=kOutput, calls=%fused_computation.23.clone.1 | convolution fusion | flops 1610620928 | bytes 16777216 | tf_op jit(solution)/shard_map/while/body/eval_jaxpr/dot_general | solution.py:57
  117.6 136.5 %all-gather.13.cloned.1.call-done = bf16[8192,2048]{1,0:T(8,128)(2,1)} async-done(((bf16[1024,2048]{1,0:T(8,128)(2,1)}), bf16[8192,2048]{1,0:T(8,128)(2,1)}) %all-gather.13.cloned.1.call-update) | async-done | bytes 33554448 | tf_op jit(solution)/shard_map/all_gather | solution.py:70
  254.1 17.9 %convert_multiply_fusion.4 = (f32[256,2048]{1,0:T(8,128)}, f32[256,2048]{1,0:T(8,128)}) fusion(bf16[256,2048]{1,0:T(8,128)(2,1)} %param.16, bf16[256,8192]{1,0:T(8,128)(2,1)} %all-gather.11.cloned.1.call-done, bf16[8192,2048]{1,0:T(8,128)(2,1)} %all-gather.13.cloned.1.call-done), kind=kOutput, calls=%fused_computation.57 | convolution fusion | flops 8590983168 | bytes 42991616 | tf_op jit(solution)/shard_map/dot_general | solution.py:68
  274.3 343.8 %while.68 = (s32[]{:T(128)}, f32[16,2048]{1,0:T(8,128)}, f32[16,2048]{1,0:T(8,128)}, f32[4,64,2048]{2,1,0:T(8,128)}, f32[4,64,2048]{2,1,0:T(8,128)}, /*index=5*/...) while((s32[]{:T(128)}, f32[16,2048]{1,0:T(8,128)}, ...), condition=%wide.region_9.10_spmd.clone.clone.clone, body=%wide.region_6.0_spmd.clone.clone.clone.sunk | while | flops 1639882752 | bytes 212862208 | solution.py:86
  283.5 8.8 %fusion.55 = f32[32768,64]{0,1:T(8,128)S(1)} fusion(f32[64,32768]{1,0:T(8,128)S(1)} %bitcast.144), kind=kOutput, calls=%fused_computation.41.clone.1 | convolution fusion | flops 1610620928 | bytes 16777216 | tf_op jit(solution)/shard_map/while/body/eval_jaxpr/dot_general | solution.py:79
  300.3 10.9 %multiply_reduce_fusion.7 = (f32[64,2048]{1,0:T(8,128)S(1)}, f32[64,16,2048]{2,1,0:T(8,128)}, f32[64,16,2048]{2,1,0:T(8,128)S(1)}, f32[64,16,2048]{2,1,0:T(8,128)}) fusion(f32[16,2048]{1,0:T(8,128)} %copy-done.7, f32[16,2048]{1,0:T(8,128)} %get-tuple-element.1005, f32[64]{0:T(128)S(1)} %get-tuple-element.1028, f32[16,2048]{1,0:T(8,128)} %copy-done, ...), kind=kLoop, calls=%fused_computation.35.clone.1 | loop fusion | flops 14548992 | bytes 34603520 | tf_op jit(solution)/shard_map/while/body/eval_jaxpr/reduce_sum | solution.py:84
  317.1 11.7 %copy.32 = f32[8,8,16,2048]{3,1,2,0:T(8,128)} copy(f32[8,8,16,2048]{3,2,1,0:T(8,128)} %bitcast.149) | data formatting | bytes 16777216 | tf_op jit(solution)/shard_map/while
  328.7 11.7 %copy.33 = f32[8,8,16,2048]{3,1,2,0:T(8,128)} copy(f32[8,8,16,2048]{3,2,1,0:T(8,128)} %bitcast.146) | data formatting | bytes 16777216 | tf_op jit(solution)/shard_map/while
  348.6 9.5 %fusion.56 = f32[32768]{0:T(1024)S(1)} fusion(f32[64,32768]{1,0:T(8,128)} %bitcast.150, f32[64,32768]{1,0:T(8,128)} %bitcast.151, f32[32768,64]{0,1:T(8,128)S(1)} %fusion.55, f32[64,32768]{1,0:T(8,128)} %bitcast.152, f32[32768]{0:T(1024)S(1)} %bitcast.154), kind=kLoop, calls=%fused_computation.31.clone.1 | loop fusion | flops 10452992 | bytes 33816576 | tf_op jit(solution)/shard_map/while/body/eval_jaxpr/reduce_sum | solution.py:83
  368.4 9.0 %fusion.55 = f32[32768,64]{0,1:T(8,128)S(1)} fusion(f32[64,32768]{1,0:T(8,128)S(1)} %bitcast.144), kind=kOutput, calls=%fused_computation.41.clone.1 | convolution fusion | flops 1610620928 | bytes 16777216 | tf_op jit(solution)/shard_map/while/body/eval_jaxpr/dot_general | solution.py:79
  385.4 10.7 %multiply_reduce_fusion.7 = (f32[64,2048]{1,0:T(8,128)S(1)}, f32[64,16,2048]{2,1,0:T(8,128)}, f32[64,16,2048]{2,1,0:T(8,128)S(1)}, f32[64,16,2048]{2,1,0:T(8,128)}) fusion(f32[16,2048]{1,0:T(8,128)} %copy-done.7, f32[16,2048]{1,0:T(8,128)} %get-tuple-element.1005, f32[64]{0:T(128)S(1)} %get-tuple-element.1028, f32[16,2048]{1,0:T(8,128)} %copy-done, ...), kind=kLoop, calls=%fused_computation.35.clone.1 | loop fusion | flops 14548992 | bytes 34603520 | tf_op jit(solution)/shard_map/while/body/eval_jaxpr/reduce_sum | solution.py:84
  402.0 11.7 %copy.32 = f32[8,8,16,2048]{3,1,2,0:T(8,128)} copy(f32[8,8,16,2048]{3,2,1,0:T(8,128)} %bitcast.149) | data formatting | bytes 16777216 | tf_op jit(solution)/shard_map/while
  413.6 11.7 %copy.33 = f32[8,8,16,2048]{3,1,2,0:T(8,128)} copy(f32[8,8,16,2048]{3,2,1,0:T(8,128)} %bitcast.146) | data formatting | bytes 16777216 | tf_op jit(solution)/shard_map/while
  433.6 9.5 %fusion.56 = f32[32768]{0:T(1024)S(1)} fusion(f32[64,32768]{1,0:T(8,128)} %bitcast.150, f32[64,32768]{1,0:T(8,128)} %bitcast.151, f32[32768,64]{0,1:T(8,128)S(1)} %fusion.55, f32[64,32768]{1,0:T(8,128)} %bitcast.152, f32[32768]{0:T(1024)S(1)} %bitcast.154), kind=kLoop, calls=%fused_computation.31.clone.1 | loop fusion | flops 10452992 | bytes 33816576 | tf_op jit(solution)/shard_map/while/body/eval_jaxpr/reduce_sum | solution.py:83
  453.5 8.8 %fusion.55 = f32[32768,64]{0,1:T(8,128)S(1)} fusion(f32[64,32768]{1,0:T(8,128)S(1)} %bitcast.144), kind=kOutput, calls=%fused_computation.41.clone.1 | convolution fusion | flops 1610620928 | bytes 16777216 | tf_op jit(solution)/shard_map/while/body/eval_jaxpr/dot_general | solution.py:79
  470.2 10.7 %multiply_reduce_fusion.7 = (f32[64,2048]{1,0:T(8,128)S(1)}, f32[64,16,2048]{2,1,0:T(8,128)}, f32[64,16,2048]{2,1,0:T(8,128)S(1)}, f32[64,16,2048]{2,1,0:T(8,128)}) fusion(f32[16,2048]{1,0:T(8,128)} %copy-done.7, f32[16,2048]{1,0:T(8,128)} %get-tuple-element.1005, f32[64]{0:T(128)S(1)} %get-tuple-element.1028, f32[16,2048]{1,0:T(8,128)} %copy-done, ...), kind=kLoop, calls=%fused_computation.35.clone.1 | loop fusion | flops 14548992 | bytes 34603520 | tf_op jit(solution)/shard_map/while/body/eval_jaxpr/reduce_sum | solution.py:84
  486.8 11.7 %copy.32 = f32[8,8,16,2048]{3,1,2,0:T(8,128)} copy(f32[8,8,16,2048]{3,2,1,0:T(8,128)} %bitcast.149) | data formatting | bytes 16777216 | tf_op jit(solution)/shard_map/while
  498.5 11.7 %copy.33 = f32[8,8,16,2048]{3,1,2,0:T(8,128)} copy(f32[8,8,16,2048]{3,2,1,0:T(8,128)} %bitcast.146) | data formatting | bytes 16777216 | tf_op jit(solution)/shard_map/while
  518.6 9.5 %fusion.56 = f32[32768]{0:T(1024)S(1)} fusion(f32[64,32768]{1,0:T(8,128)} %bitcast.150, f32[64,32768]{1,0:T(8,128)} %bitcast.151, f32[32768,64]{0,1:T(8,128)S(1)} %fusion.55, f32[64,32768]{1,0:T(8,128)} %bitcast.152, f32[32768]{0:T(1024)S(1)} %bitcast.154), kind=kLoop, calls=%fused_computation.31.clone.1 | loop fusion | flops 10452992 | bytes 33816576 | tf_op jit(solution)/shard_map/while/body/eval_jaxpr/reduce_sum | solution.py:83
  538.3 8.8 %fusion.55 = f32[32768,64]{0,1:T(8,128)S(1)} fusion(f32[64,32768]{1,0:T(8,128)S(1)} %bitcast.144), kind=kOutput, calls=%fused_computation.41.clone.1 | convolution fusion | flops 1610620928 | bytes 16777216 | tf_op jit(solution)/shard_map/while/body/eval_jaxpr/dot_general | solution.py:79
  555.1 10.9 %multiply_reduce_fusion.7 = (f32[64,2048]{1,0:T(8,128)S(1)}, f32[64,16,2048]{2,1,0:T(8,128)}, f32[64,16,2048]{2,1,0:T(8,128)S(1)}, f32[64,16,2048]{2,1,0:T(8,128)}) fusion(f32[16,2048]{1,0:T(8,128)} %copy-done.7, f32[16,2048]{1,0:T(8,128)} %get-tuple-element.1005, f32[64]{0:T(128)S(1)} %get-tuple-element.1028, f32[16,2048]{1,0:T(8,128)} %copy-done, ...), kind=kLoop, calls=%fused_computation.35.clone.1 | loop fusion | flops 14548992 | bytes 34603520 | tf_op jit(solution)/shard_map/while/body/eval_jaxpr/reduce_sum | solution.py:84
  571.9 11.7 %copy.32 = f32[8,8,16,2048]{3,1,2,0:T(8,128)} copy(f32[8,8,16,2048]{3,2,1,0:T(8,128)} %bitcast.149) | data formatting | bytes 16777216 | tf_op jit(solution)/shard_map/while
  583.5 11.7 %copy.33 = f32[8,8,16,2048]{3,1,2,0:T(8,128)} copy(f32[8,8,16,2048]{3,2,1,0:T(8,128)} %bitcast.146) | data formatting | bytes 16777216 | tf_op jit(solution)/shard_map/while
  603.4 9.5 %fusion.56 = f32[32768]{0:T(1024)S(1)} fusion(f32[64,32768]{1,0:T(8,128)} %bitcast.150, f32[64,32768]{1,0:T(8,128)} %bitcast.151, f32[32768,64]{0,1:T(8,128)S(1)} %fusion.55, f32[64,32768]{1,0:T(8,128)} %bitcast.152, f32[32768]{0:T(1024)S(1)} %bitcast.154), kind=kLoop, calls=%fused_computation.31.clone.1 | loop fusion | flops 10452992 | bytes 33816576 | tf_op jit(solution)/shard_map/while/body/eval_jaxpr/reduce_sum | solution.py:83
  618.3 13.6 %while.65 = (s32[]{:T(128)}, f32[16,2048]{1,0:T(8,128)}, s32[]{:T(128)}, f32[8,16,2048]{2,1,0:T(8,128)}, f32[8,16,2048]{2,1,0:T(8,128)}, /*index=5*/s32[]{:T(128)}, s32[]{:T(128)}) while((s32[]{:T(128)}, f32[16,2048]{1,0:T(8,128)}, s32[]{:T(128)}, f32[8,16,2048]{2,1,0:T(8,128)}, f32[8,16,2048]{2,1,0:T(8,128)}, ...), condition=%wide.region_4.5_spmd.clone, body=%wide.region_3.4_spmd.clone.sunk | while | flops 131076 | bytes 524397 | solution.py:23
  631.8 9.8 %all-gather.19.cloned.1.call-done = f32[128,2048]{1,0:T(8,128)} async-done(((f32[16,2048]{1,0:T(8,128)}), f32[128,2048]{1,0:T(8,128)}) %all-gather.19.cloned.1.call-update) | async-done | bytes 1048592 | tf_op jit(solution)/shard_map/all_gather | solution.py:10
  641.7 13.5 %while.66 = (s32[]{:T(128)}, f32[16,2048]{1,0:T(8,128)}, s32[]{:T(128)}, f32[8,16,2048]{2,1,0:T(8,128)}, f32[8,16,2048]{2,1,0:T(8,128)}, /*index=5*/s32[]{:T(128)}, s32[]{:T(128)}, s32[]{:T(128)}, s32[]{:T(128)}) while((s32[]{:T(128)}, f32[16,2048]{1,0:T(8,128)}, s32[]{:T(128)}, f32[8,16,2048]{2,1,0:T(8,128)}, ...), condition=%wide.region_11.12_spmd.clone, body=%wide.region_10.11_spmd.clone.sunk | while | flops 131080 | bytes 524459 | solution.py:23
  657.1 21.9 %multiply_reduce_fusion.2 = (f32[256,2048]{1,0:T(8,128)S(1)}, f32[256,2048]{1,0:T(8,128)S(1)}) fusion(f32[16,2048]{1,0:T(8,128)S(1)} %get-tuple-element.781, f32[256]{0:T(256)S(1)} %copy-done.20, f32[16,2048]{1,0:T(8,128)S(1)} %get-tuple-element.1117, f32[16,2048]{1,0:T(8,128)S(1)} %get-tuple-element.782, f32[256]{0:T(256)} %convert_add_fusion), kind=kLoop, calls=%fused_computation.44 | loop fusion | flops 49283072 | bytes 4589568 | tf_op jit(solution)/shard_map/reduce_sum | solution.py:104
  (229 shorter events, 239.9 us)
Async XLA Ops:
  7.2 110.4 %all-gather.11.cloned.1.call-start = ((), (), s32[]{:S(2)}) async-start(), calls=%async_computation | async-start | bytes 5242880 | tf_op jit(solution)/shard_map/all_gather | solution.py:67
  7.9 246.2 %all-gather.13.cloned.1.call-start = ((), (), s32[]{:S(2)}) async-start(), calls=%async_computation.1 | async-start | bytes 37748736 | tf_op jit(solution)/shard_map/all_gather | solution.py:70
  8.7 609.6 %all-gather.15.cloned.1.call-start = ((), (), s32[]{:S(2)}) async-start(), calls=%async_computation.2 | async-start | bytes 1179648 | tf_op jit(solution)/shard_map/all_gather | solution.py:10
  10.5 607.8 %all-gather.17.cloned.1.call-start = ((), (), s32[]{:S(2)}) async-start(), calls=%async_computation.3 | async-start | bytes 1179648 | tf_op jit(solution)/shard_map/all_gather | solution.py:10
  116.3 525.3 %all-gather.19.cloned.1.call-start = ((), (), s32[]{:S(2)}) async-start(), calls=%async_computation.4 | async-start | bytes 1179648 | tf_op jit(solution)/shard_map/all_gather | solution.py:10
  274.3 382.8 %copy-start.20 = (f32[256]{0:T(256)S(1)}, f32[256]{0:T(256)}, u32[]{:S(2)}) copy-start(f32[256]{0:T(256)} %convert_subtract_fusion) | copy-start | bytes 3076
  348.6 9.5 %copy-start.13 = (f32[16,2048]{1,0:T(8,128)S(1)}, f32[16,2048]{1,0:T(8,128)}, u32[]{:S(2)}) copy-start(f32[16,2048]{1,0:T(8,128)} %get-tuple-element.1006) | copy-start | bytes 393220 | tf_op jit(solution)/shard_map/while
  348.6 10.5 %copy-start.1 = (f32[16,2048]{1,0:T(8,128)S(1)}, f32[16,2048]{1,0:T(8,128)}, u32[]{:S(2)}) copy-start(f32[16,2048]{1,0:T(8,128)} %copy-done) | copy-start | bytes 393220 | tf_op jit(solution)/shard_map/while
  348.6 10.5 %copy-start.3 = (f32[4,64,2048]{2,1,0:T(8,128)S(1)}, f32[4,64,2048]{2,1,0:T(8,128)}, u32[]{:S(2)}) copy-start(f32[4,64,2048]{2,1,0:T(8,128)} %copy-done.2) | copy-start | bytes 6291460 | tf_op jit(solution)/shard_map/while
  348.6 10.5 %copy-start.6 = (f32[16,2048]{1,0:T(8,128)S(1)}, f32[16,2048]{1,0:T(8,128)}, u32[]{:S(2)}) copy-start(f32[16,2048]{1,0:T(8,128)} %copy-done.5) | copy-start | bytes 393220 | tf_op jit(solution)/shard_map/while
  348.6 10.5 %copy-start.8 = (f32[16,2048]{1,0:T(8,128)S(1)}, f32[16,2048]{1,0:T(8,128)}, u32[]{:S(2)}) copy-start(f32[16,2048]{1,0:T(8,128)} %copy-done.7) | copy-start | bytes 393220 | tf_op jit(solution)/shard_map/while
  433.5 9.5 %copy-start.13 = (f32[16,2048]{1,0:T(8,128)S(1)}, f32[16,2048]{1,0:T(8,128)}, u32[]{:S(2)}) copy-start(f32[16,2048]{1,0:T(8,128)} %get-tuple-element.1006) | copy-start | bytes 393220 | tf_op jit(solution)/shard_map/while
  433.5 10.5 %copy-start.1 = (f32[16,2048]{1,0:T(8,128)S(1)}, f32[16,2048]{1,0:T(8,128)}, u32[]{:S(2)}) copy-start(f32[16,2048]{1,0:T(8,128)} %copy-done) | copy-start | bytes 393220 | tf_op jit(solution)/shard_map/while
  433.5 10.5 %copy-start.3 = (f32[4,64,2048]{2,1,0:T(8,128)S(1)}, f32[4,64,2048]{2,1,0:T(8,128)}, u32[]{:S(2)}) copy-start(f32[4,64,2048]{2,1,0:T(8,128)} %copy-done.2) | copy-start | bytes 6291460 | tf_op jit(solution)/shard_map/while
  433.5 10.5 %copy-start.6 = (f32[16,2048]{1,0:T(8,128)S(1)}, f32[16,2048]{1,0:T(8,128)}, u32[]{:S(2)}) copy-start(f32[16,2048]{1,0:T(8,128)} %copy-done.5) | copy-start | bytes 393220 | tf_op jit(solution)/shard_map/while
  433.5 10.5 %copy-start.8 = (f32[16,2048]{1,0:T(8,128)S(1)}, f32[16,2048]{1,0:T(8,128)}, u32[]{:S(2)}) copy-start(f32[16,2048]{1,0:T(8,128)} %copy-done.7) | copy-start | bytes 393220 | tf_op jit(solution)/shard_map/while
  518.6 9.5 %copy-start.13 = (f32[16,2048]{1,0:T(8,128)S(1)}, f32[16,2048]{1,0:T(8,128)}, u32[]{:S(2)}) copy-start(f32[16,2048]{1,0:T(8,128)} %get-tuple-element.1006) | copy-start | bytes 393220 | tf_op jit(solution)/shard_map/while
  518.6 10.4 %copy-start.1 = (f32[16,2048]{1,0:T(8,128)S(1)}, f32[16,2048]{1,0:T(8,128)}, u32[]{:S(2)}) copy-start(f32[16,2048]{1,0:T(8,128)} %copy-done) | copy-start | bytes 393220 | tf_op jit(solution)/shard_map/while
  518.6 10.4 %copy-start.3 = (f32[4,64,2048]{2,1,0:T(8,128)S(1)}, f32[4,64,2048]{2,1,0:T(8,128)}, u32[]{:S(2)}) copy-start(f32[4,64,2048]{2,1,0:T(8,128)} %copy-done.2) | copy-start | bytes 6291460 | tf_op jit(solution)/shard_map/while
  518.6 10.4 %copy-start.6 = (f32[16,2048]{1,0:T(8,128)S(1)}, f32[16,2048]{1,0:T(8,128)}, u32[]{:S(2)}) copy-start(f32[16,2048]{1,0:T(8,128)} %copy-done.5) | copy-start | bytes 393220 | tf_op jit(solution)/shard_map/while
  518.6 10.4 %copy-start.8 = (f32[16,2048]{1,0:T(8,128)S(1)}, f32[16,2048]{1,0:T(8,128)}, u32[]{:S(2)}) copy-start(f32[16,2048]{1,0:T(8,128)} %copy-done.7) | copy-start | bytes 393220 | tf_op jit(solution)/shard_map/while
  603.4 10.5 %copy-start.1 = (f32[16,2048]{1,0:T(8,128)S(1)}, f32[16,2048]{1,0:T(8,128)}, u32[]{:S(2)}) copy-start(f32[16,2048]{1,0:T(8,128)} %copy-done) | copy-start | bytes 393220 | tf_op jit(solution)/shard_map/while
  603.4 10.5 %copy-start.3 = (f32[4,64,2048]{2,1,0:T(8,128)S(1)}, f32[4,64,2048]{2,1,0:T(8,128)}, u32[]{:S(2)}) copy-start(f32[4,64,2048]{2,1,0:T(8,128)} %copy-done.2) | copy-start | bytes 6291460 | tf_op jit(solution)/shard_map/while
  603.4 10.5 %copy-start.6 = (f32[16,2048]{1,0:T(8,128)S(1)}, f32[16,2048]{1,0:T(8,128)}, u32[]{:S(2)}) copy-start(f32[16,2048]{1,0:T(8,128)} %copy-done.5) | copy-start | bytes 393220 | tf_op jit(solution)/shard_map/while
  603.4 10.5 %copy-start.8 = (f32[16,2048]{1,0:T(8,128)S(1)}, f32[16,2048]{1,0:T(8,128)}, u32[]{:S(2)}) copy-start(f32[16,2048]{1,0:T(8,128)} %copy-done.7) | copy-start | bytes 393220 | tf_op jit(solution)/shard_map/while
  618.2 64.0 %all-gather.21.cloned.1.call-start = ((), (), s32[]{:S(2)}) async-start(), calls=%async_computation.5 | async-start | bytes 1179648 | tf_op jit(solution)/shard_map/all_gather | solution.py:33
  657.1 22.0 %copy-start.11 = (f32[4,64,2048]{2,1,0:T(8,128)S(1)}, f32[4,64,2048]{2,1,0:T(8,128)}, u32[]{:S(2)}) copy-start(f32[4,64,2048]{2,1,0:T(8,128)} %get-tuple-element.500) | copy-start | bytes 6291460
  657.1 22.0 %copy-start.12 = (f32[4,64,2048]{2,1,0:T(8,128)S(1)}, f32[4,64,2048]{2,1,0:T(8,128)}, u32[]{:S(2)}) copy-start(f32[4,64,2048]{2,1,0:T(8,128)} %get-tuple-element.497) | copy-start | bytes 6291460
  657.1 22.0 %copy-start.15 = (bf16[256,2048]{1,0:T(8,128)(2,1)S(1)}, bf16[256,2048]{1,0:T(8,128)(2,1)}, u32[]{:S(2)}) copy-start(bf16[256,2048]{1,0:T(8,128)(2,1)} %param.17) | copy-start | bytes 3145732
  657.1 22.0 %copy-start.16 = (bf16[256,2048]{1,0:T(8,128)(2,1)S(1)}, bf16[256,2048]{1,0:T(8,128)(2,1)}, u32[]{:S(2)}) copy-start(bf16[256,2048]{1,0:T(8,128)(2,1)} %param.18) | copy-start | bytes 3145732
  657.1 22.0 %copy-start.17 = (f32[256,2048]{1,0:T(8,128)S(1)}, f32[256,2048]{1,0:T(8,128)}, u32[]{:S(2)}) copy-start(f32[256,2048]{1,0:T(8,128)} %get-tuple-element.788) | copy-start | bytes 6291460
  657.1 22.0 %copy-start.19 = (f32[256]{0:T(256)S(1)}, f32[256]{0:T(256)}, u32[]{:S(2)}) copy-start(f32[256]{0:T(256)} %copy-done.18) | copy-start | bytes 3076
  (28 other events, 124.1 us)
Sparse Core Ops, SparseCore 0:
  9.6 83.4 all-gather.10
  94.9 159.1 all-gather.12
  256.6 23.3 all-gather.14
  282.3 23.3 all-gather.16
  618.3 23.3 all-gather.18
  657.2 23.3 all-gather.20
